TPU v7x, 256 devices: a whole 4x4x8 slice. The times are simulated.
256 devices in a mesh: row: 16 (over z, y_hi), col: 16 (over y_lo, x, core).
Axes of the slice: x: 4, y: 4 (y_hi: 2, y_lo: 2; y = y_hi * 2 + y_lo), z: 8, core: 2. Of those that a mesh axis runs over, the one named last changes fastest.
Arguments:
- object_field: float32 [2, 4096, 4096], P(None, 'row', 'col'), may hold values from -5 to 5
- probe: float32 [2, 256, 256], replicated, may hold values from -6 to 6
- amplitudes: float32 [16, 16, 4, 256, 256], P('row', 'col'), may hold values from 0 to 11, as said below
- positions: int32 [16, 16, 4, 2], P('row', 'col'), may hold values from 0 to 64
Outputs:
- object_next: float32 [2, 4096, 4096], P(None, 'row', 'col')
- probe_next: float32 [2, 256, 256], replicated
Inputs may be any that keep to these rules, and one draw needn't show every extreme that they name: Positive amplitudes.
All inputs are finite; a program needn't handle non-finite values.
Results may differ from a plain program's by a relative error of at most 0.0003.
Values sent between devices are 32-bit elements; how exact they have to be, the bound alone decides.
A program may use at most 64 MiB of HBM per device.

v0:
```python
import math
import jax
import jax.numpy as jnp
from jax import lax
from jax.sharding import PartitionSpec as P

W = 256
MARGIN = 32
smoothing = 0.1
regular = 1.0
epsilon = 1e-06


def padded(block, sides, width):
    for axis, dim in sides:
        count = lax.axis_size(axis)
        forward = [(i, i + 1) for i in range(count - 1)]
        backward = [(target, source) for source, target in forward]
        low = lax.ppermute(
            lax.slice_in_dim(block, block.shape[dim] - width, None, axis=dim), axis, forward
        )
        high = lax.ppermute(lax.slice_in_dim(block, 0, width, axis=dim), axis, backward)
        block = jnp.concatenate([low, block, high], axis=dim)
    return block


def shifted(block, axis, distance):
    devices = range(lax.axis_size(axis))
    route = [(i - distance, i) for i in devices if i - distance in devices]
    return lax.ppermute(block, axis, route)


def tables(length):
    indices = jnp.arange(length, dtype=jnp.int32)
    phases = (indices[:, None] * indices[None, :] % length).astype(jnp.float32) * (
        2.0 * math.pi / length
    )
    scaling = 1.0 / math.sqrt(length)
    cosine = jnp.cos(phases) * scaling
    sines = jnp.sin(phases) * scaling
    forward = jnp.concatenate(
        [jnp.concatenate([cosine, sines], 1), jnp.concatenate([-sines, cosine], 1)], 0
    )
    inverse = jnp.concatenate(
        [jnp.concatenate([cosine, -sines], 1), jnp.concatenate([sines, cosine], 1)], 0
    )
    return (forward, inverse)


def transform(wavefield, left_matrix, right_matrix):
    length = wavefield.shape[1]
    stacked = wavefield.reshape(2 * length, length)
    mixed = jnp.dot(left_matrix, stacked, precision=lax.Precision.HIGHEST)
    paired = jnp.concatenate([mixed[:length], mixed[length:]], axis=1)
    result = jnp.dot(paired, right_matrix, precision=lax.Precision.HIGHEST)
    return jnp.stack([result[:, :length], result[:, length:]])


def frame_terms(probe, window, amplitude, forward, inverse):
    exit_real = probe[0] * window[0] - probe[1] * window[1]
    exit_imag = probe[0] * window[1] + probe[1] * window[0]
    wave = jnp.stack([exit_real, exit_imag])
    far_field = transform(wave, forward, inverse)
    factor = amplitude / jnp.sqrt(
        far_field[0] * far_field[0] + far_field[1] * far_field[1] + smoothing
    )
    near_field = transform(far_field * factor[None], inverse, forward)
    difference = near_field - wave
    object_real = probe[0] * difference[0] + probe[1] * difference[1]
    object_imag = probe[0] * difference[1] - probe[1] * difference[0]
    probe_real = window[0] * difference[0] + window[1] * difference[1]
    probe_imag = window[0] * difference[1] - window[1] * difference[0]
    window_power = window[0] * window[0] + window[1] * window[1]
    return (
        jnp.stack([object_real, object_imag]),
        jnp.stack([probe_real, probe_imag, window_power]),
    )


def add_edges(middle, leading, trailing, along, tile_side, margin):
    head_pad = [(0, 0), (0, 0), (0, 0)]
    tail_pad = [(0, 0), (0, 0), (0, 0)]
    head_pad[along] = (0, tile_side - margin)
    tail_pad[along] = (tile_side - margin, 0)
    return middle + jnp.pad(leading, head_pad) + jnp.pad(trailing, tail_pad)


def per_device(object_field, probe, amplitudes, positions):
    forward, inverse = tables(W)
    tile_side = object_field.shape[1]
    margin = MARGIN
    window_side = tile_side + 2 * margin
    extended = padded(object_field, (("row", 1), ("col", 2)), MARGIN)
    power_map = probe[0] * probe[0] + probe[1] * probe[1]
    measured = amplitudes[0, 0]
    offsets = positions[0, 0]
    frame_total = measured.shape[0]
    anchor = jnp.zeros((), jnp.int32)

    def visit(frame_index, carried):
        canvas, probe_acc = carried
        amplitude = measured[frame_index]
        offset = offsets[frame_index]
        window = lax.dynamic_slice(extended, (anchor, offset[0], offset[1]), (2, W, W))
        object_term, probe_term = frame_terms(probe, window, amplitude, forward, inverse)
        update = jnp.concatenate([object_term, power_map[None]], 0)
        current = lax.dynamic_slice(canvas, (anchor, offset[0], offset[1]), (3, W, W))
        canvas = lax.dynamic_update_slice(canvas, current + update, (anchor, offset[0], offset[1]))
        return (canvas, probe_acc + probe_term)

    canvas_start = jnp.zeros((3, window_side, window_side), jnp.float32)
    probe_start = jnp.zeros((3, W, W), jnp.float32)
    canvas, probe_acc = lax.fori_loop(0, frame_total, visit, (canvas_start, probe_start))
    from_above = shifted(canvas[:, window_side - margin :, :], "row", 1)
    from_below = shifted(canvas[:, :margin, :], "row", -1)
    row_folded = add_edges(
        canvas[:, margin : margin + tile_side, :], from_above, from_below, 1, tile_side, margin
    )
    from_before = shifted(row_folded[:, :, window_side - margin :], "col", 1)
    from_after = shifted(row_folded[:, :, :margin], "col", -1)
    folded = add_edges(
        row_folded[:, :, margin : margin + tile_side], from_before, from_after, 2, tile_side, margin
    )
    object_next = object_field + folded[0:2] / (folded[2] + regular)
    local_target = jnp.sum(measured * measured)
    devices = lax.axis_size("row") * lax.axis_size("col")
    frame_count = frame_total * devices
    totals, target_sum = lax.psum((probe_acc, local_target), ("row", "col"))
    stepped = probe + totals[0:2] / (totals[2] + regular)
    probe_power = jnp.sum(stepped * stepped)
    target = target_sum / frame_count
    probe_next = stepped * jnp.sqrt(target / (probe_power + epsilon))
    return (object_next, probe_next)


def solution(mesh):
    return jax.shard_map(
        per_device,
        mesh=mesh,
        in_specs=(
            P(None, "row", "col"),
            P(),
            P("row", "col", None, None, None),
            P("row", "col", None, None),
        ),
        out_specs=(P(None, "row", "col"), P()),
        check_vma=False,
    )
```

profile of v0, /device:TPU:2, one launch (start us, length us, event | category | flops | bytes accessed | tf_op | source)
XLA Modules:
  0.0 516.5 jit_solution(1246306254406606753)
XLA Ops:
  8.2 5.1 collective-permute-start
  15.6 1.8 add_bitcast_fusion
  18.5 2.5 collective-permute-done.1
  21.9 1.9 collective-permute-start.2
  23.8 3.6 collective-permute-start.3
  27.7 2.9 collective-permute-done.2
  30.6 1.8 collective-permute-done.3
  32.3 2.4 pad_maximum_fusion.5
  36.0 107.6 %while.16 = (s32[]{:T(128)}, f32[3,320,320]{2,1,0:T(8,128)}, f32[3,256,256]{2,1,0:T(8,128)}, s32[4,2]{0,1:T(2,128)S(1)}, f32[2,256,256]{2,1,0:T(8,128)S(1)}, /*i...) while((s32[]{:T(128)}, f32[3,320,320]{2,1,0:T(8,128)}, ...), condition=%wide.region_1.2_spmd.clone, body=%wide.region_0.1_spmd.clone.sunk | while | flops 3225354240 | bytes 31064388 | solution.py:113
  41.9 1.9 convolution_bitcast_fusion.4
  45.9 1.9 convolution_bitcast_fusion.5
  51.4 2.9 maximum_add_fusion.3
  54.3 8.7 %dynamic_update_slice.9 = f32[3,320,320]{2,1,0:T(8,128)} dynamic-update-slice(f32[3,320,320]{2,1,0:T(8,128)} %get-tuple-element.377, f32[3,256,256]{2,1,0:T(8,128)S(1)} %get-tuple-element.360, s32[]{:T(128)} %constant.57.clone.1..sunk, s32[]{:T(128)S(6)} %select_n.61, s32[]{:T(128)S(6)} %select_n.62) | dynamic-update-slice | bytes 1572868 | tf_op jit(solution)/shard_map/while/body/eval_jaxpr/dynamic_update_slice | solution.py:108
  68.9 1.9 convolution_bitcast_fusion.4
  73.0 1.9 convolution_bitcast_fusion.5
  78.5 3.2 maximum_add_fusion.3
  81.7 8.5 %dynamic_update_slice.9 = f32[3,320,320]{2,1,0:T(8,128)} dynamic-update-slice(f32[3,320,320]{2,1,0:T(8,128)} %get-tuple-element.377, f32[3,256,256]{2,1,0:T(8,128)S(1)} %get-tuple-element.360, s32[]{:T(128)} %constant.57.clone.1..sunk, s32[]{:T(128)S(6)} %select_n.61, s32[]{:T(128)S(6)} %select_n.62) | dynamic-update-slice | bytes 1572868 | tf_op jit(solution)/shard_map/while/body/eval_jaxpr/dynamic_update_slice | solution.py:108
  96.1 1.9 convolution_bitcast_fusion.4
  100.1 1.9 convolution_bitcast_fusion.5
  105.6 3.2 maximum_add_fusion.3
  108.8 8.5 %dynamic_update_slice.9 = f32[3,320,320]{2,1,0:T(8,128)} dynamic-update-slice(f32[3,320,320]{2,1,0:T(8,128)} %get-tuple-element.377, f32[3,256,256]{2,1,0:T(8,128)S(1)} %get-tuple-element.360, s32[]{:T(128)} %constant.57.clone.1..sunk, s32[]{:T(128)S(6)} %select_n.61, s32[]{:T(128)S(6)} %select_n.62) | dynamic-update-slice | bytes 1572868 | tf_op jit(solution)/shard_map/while/body/eval_jaxpr/dynamic_update_slice | solution.py:108
  123.2 1.9 convolution_bitcast_fusion.4
  127.3 1.9 convolution_bitcast_fusion.5
  132.7 3.2 maximum_add_fusion.3
  135.9 7.6 %dynamic_update_slice.9 = f32[3,320,320]{2,1,0:T(8,128)} dynamic-update-slice(f32[3,320,320]{2,1,0:T(8,128)} %get-tuple-element.377, f32[3,256,256]{2,1,0:T(8,128)S(1)} %get-tuple-element.360, s32[]{:T(128)} %constant.57.clone.1..sunk, s32[]{:T(128)S(6)} %select_n.61, s32[]{:T(128)S(6)} %select_n.62) | dynamic-update-slice | bytes 1572868 | tf_op jit(solution)/shard_map/while/body/eval_jaxpr/dynamic_update_slice | solution.py:108
  144.5 5.3 %collective-permute-start.4 = (f32[3,32,320]{2,1,0:T(8,128)S(1)}, f32[3,32,320]{2,1,0:T(8,128)S(1)}, u32[]{:S(2)}, u32[]{:S(2)}) collective-permute-start(f32[3,32,320]{2,1,0:T(8,128)S(1)} %get-tuple-element.249), channel_id=1, source_target_pairs={{0,16},{16,32},{32,48},{48,64},{64,80},{80,96},{96,112},{112,128},... | collective-permute-start | bytes 368648 | tf_op jit(solution)/shard_map/ppermute | solution.py:30
  152.9 6.3 %collective-permute-done.5 = f32[3,32,320]{2,1,0:T(8,128)S(1)} collective-permute-done((f32[3,32,320]{2,1,0:T(8,128)S(1)}, f32[3,32,320]{2,1,0:T(8,128)S(1)}, u32[]{:S(2)}, u32[]{:S(2)}) %collective-permute-start.5) | collective-permute-done | bytes 122912 | tf_op jit(solution)/shard_map/ppermute | solution.py:30
  160.8 2.6 collective-permute-start.6
  163.4 3.0 collective-permute-start.7
  167.3 81.6 %psum.15 = f32[]{:T(128)} all-reduce(f32[]{:T(128)} %multiply_reduce_fusion), channel_id=1, replica_groups=mesh['row'=16,'col'=16] {'row','col'}, use_global_device_ids=true, to_apply=%region_4.5 | all-reduce | flops 1 | bytes 8 | tf_op jit(solution)/shard_map/psum | solution.py:128
  251.4 253.7 %all-reduce.6.cloned.1.call-done = f32[3,256,256]{2,1,0:T(8,128)} async-done(((f32[3,256,256]{2,1,0:T(8,128)}), f32[3,256,256]{2,1,0:T(8,128)}) %all-reduce.6.cloned.1.call-update) | async-done | bytes 786448 | tf_op jit(solution)/shard_map/psum | solution.py:128
  506.2 1.8 multiply_reduce_fusion.1
  (99 shorter events, 47.8 us)
Async XLA Ops:
  7.2 11.3 %copy-start.3 = (f32[2,256,256]{2,1,0:T(8,128)S(1)}, f32[2,256,256]{2,1,0:T(8,128)}, u32[]{:S(2)}) copy-start(f32[2,256,256]{2,1,0:T(8,128)} %param.6) | copy-start | bytes 1572868
  7.2 498.0 %all-reduce.6.cloned.1.call-start = ((), (), s32[]{:S(2)}) async-start(), calls=%async_computation | async-start | bytes 1572864 | tf_op jit(solution)/shard_map/psum | solution.py:128
  8.2 10.2 %collective-permute-start = (f32[2,32,256]{2,1,0:T(8,128)S(1)}, f32[2,32,256]{2,1,0:T(8,128)S(1)}, u32[]{:S(2)}, u32[]{:S(2)}) collective-permute-start(f32[2,32,256]{2,1,0:T(8,128)S(1)} %get-tuple-element.258), channel_id=1, source_target_pairs={{0,16},{16,32},{32,48},{48,64},{64,80},{80,96},{96,112},{112,128},... | collective-permute-start | bytes 196616 | tf_op jit(solution)/shard_map/ppermute | solution.py:19
  13.3 7.7 %collective-permute-start.1 = (f32[2,32,256]{2,1,0:T(8,128)S(1)}, f32[2,32,256]{2,1,0:T(8,128)S(1)}, u32[]{:S(2)}, u32[]{:S(2)}) collective-permute-start(f32[2,32,256]{2,1,0:T(8,128)S(1)} %get-tuple-element.257), channel_id=1, source_target_pairs={{16,0},{32,16},{48,32},{64,48},{80,64},{96,80},{112,96},{128,112},... | collective-permute-start | bytes 196616 | tf_op jit(solution)/shard_map/ppermute | solution.py:22
  21.9 8.7 %collective-permute-start.2 = (f32[2,320,32]{2,1,0:T(8,128)}, f32[2,320,32]{2,1,0:T(8,128)}, u32[]{:S(2)}, u32[]{:S(2)}) collective-permute-start(f32[2,320,32]{2,1,0:T(8,128)} %get-tuple-element.255), channel_id=1, source_target_pairs={{0,1},{1,2},{2,3},{3,4},{4,5},{5,6},{6,7},{7,8},{8,9},{9,10},{10,1... | collective-permute-start | bytes 245768 | tf_op jit(solution)/shard_map/ppermute | solution.py:19
  23.8 8.5 %collective-permute-start.3 = (f32[2,320,32]{2,1,0:T(8,128)}, f32[2,320,32]{2,1,0:T(8,128)}, u32[]{:S(2)}, u32[]{:S(2)}) collective-permute-start(f32[2,320,32]{2,1,0:T(8,128)} %get-tuple-element.256), channel_id=1, source_target_pairs={{1,0},{2,1},{3,2},{4,3},{5,4},{6,5},{7,6},{8,7},{9,8},{10,9},{11,1... | collective-permute-start | bytes 245768 | tf_op jit(solution)/shard_map/ppermute | solution.py:22
  27.7 8.3 %copy-start = (f32[2,256,256]{2,1,0:T(8,128)S(1)}, f32[2,256,256]{2,1,0:T(8,128)}, u32[]{:S(2)}) copy-start(f32[2,256,256]{2,1,0:T(8,128)} %param.7) | copy-start | bytes 1572868
  27.7 8.3 %copy-start.6 = (s32[1,1,4,2]{2,3,1,0:T(2,128)S(1)}, s32[1,1,4,2]{2,3,1,0:T(2,128)}, u32[]{:S(2)}) copy-start(s32[1,1,4,2]{2,3,1,0:T(2,128)} %param.9) | copy-start | bytes 100
  48.9 1.2 copy-start.1
  76.0 1.2 copy-start.1
  103.1 1.2 copy-start.1
  130.2 1.2 copy-start.1
  144.5 8.4 %collective-permute-start.4 = (f32[3,32,320]{2,1,0:T(8,128)S(1)}, f32[3,32,320]{2,1,0:T(8,128)S(1)}, u32[]{:S(2)}, u32[]{:S(2)}) collective-permute-start(f32[3,32,320]{2,1,0:T(8,128)S(1)} %get-tuple-element.249), channel_id=1, source_target_pairs={{0,16},{16,32},{32,48},{48,64},{64,80},{80,96},{96,112},{112,128},... | collective-permute-start | bytes 368648 | tf_op jit(solution)/shard_map/ppermute | solution.py:30
  149.8 16.5 %copy-start.2 = (f32[4,256,256]{2,1,0:T(8,128)S(1)}, f32[4,256,256]{2,1,0:T(8,128)}, u32[]{:S(2)}) copy-start(f32[4,256,256]{2,1,0:T(8,128)} %get-tuple-element.408) | copy-start | bytes 3145732
  149.8 9.4 %collective-permute-start.5 = (f32[3,32,320]{2,1,0:T(8,128)S(1)}, f32[3,32,320]{2,1,0:T(8,128)S(1)}, u32[]{:S(2)}, u32[]{:S(2)}) collective-permute-start(f32[3,32,320]{2,1,0:T(8,128)S(1)} %get-tuple-element.250), channel_id=1, source_target_pairs={{16,0},{32,16},{48,32},{64,48},{80,64},{96,80},{112,96},{128,112},... | collective-permute-start | bytes 368648 | tf_op jit(solution)/shard_map/ppermute | solution.py:30
  160.8 88.7 %collective-permute-start.6 = (f32[3,256,32]{2,1,0:T(8,128)S(1)}, f32[3,256,32]{2,1,0:T(8,128)S(1)}, u32[]{:S(2)}, u32[]{:S(2)}) collective-permute-start(f32[3,256,32]{2,1,0:T(8,128)S(1)} %get-tuple-element.251), channel_id=1, source_target_pairs={{0,1},{1,2},{2,3},{3,4},{4,5},{5,6},{6,7},{7,8},{8,9},{9,10},{10,1... | collective-permute-start | bytes 294920 | tf_op jit(solution)/shard_map/ppermute | solution.py:30
  163.4 86.2 %collective-permute-start.7 = (f32[3,256,32]{2,1,0:T(8,128)S(1)}, f32[3,256,32]{2,1,0:T(8,128)S(1)}, u32[]{:S(2)}, u32[]{:S(2)}) collective-permute-start(f32[3,256,32]{2,1,0:T(8,128)S(1)} %get-tuple-element.252), channel_id=1, source_target_pairs={{1,0},{2,1},{3,2},{4,3},{5,4},{6,5},{7,6},{8,7},{9,8},{10,9},{11,1... | collective-permute-start | bytes 294920 | tf_op jit(solution)/shard_map/ppermute | solution.py:30
  249.5 1.0 copy-start.4
  505.2 3.6 copy-start.5
Sparse Core Ops, SparseCore 0:
  249.6 255.4 all-reduce.5
where the time goes:
time: 519 us; the launch traced here: 516 us
  waiting for transfers between devices  269 us (52%)
  blocking collectives  81.6 us (16%)
  local copies, waits for them, and re-layouts  45.4 us (9%)
  other arithmetic  41.4 us (8%)
  starting transfers between devices  24.3 us (5%)
  matrix products  23.4 us (5%)
  loops' own time  15.9 us (3%)
  between operations  15.6 us (3%)
    psum x1, waiting for transfers between devices, per_device(): totals, target_sum = lax.psum((probe_acc, local_target), ('row', 'col'))  254 us
    psum x1, blocking collectives, per_device(): totals, target_sum = lax.psum((probe_acc, local_target), ('row', 'col'))  81.6 us
    dynamic_update_slice x4, local copies, waits for them, and re-layouts, visit(): lax.dynamic_update_slice(canvas, current + update, (anchor, offset[0], of...  33.4 us
    another operation x1, loops' own time, per_device(): lax.fori_loop(0, frame_total, visit, (canvas_start, probe_start))  15.9 us
    dot_general x8, matrix products, transform(): mixed = jnp.dot(left_matrix, stacked, precision=lax.Precision.HIGHEST)  14.9 us
    add x4, other arithmetic, visit(): current + update  12.6 us
    ppermute x4, starting transfers between devices, shifted(): return lax.ppermute(block, axis, route)  12.3 us
  transfers between devices with their start and end apart: 9, of which 6 were waited for; matrix products, arithmetic and copies ran while one was open for 1% of the time, Pallas kernels for 0%

commit v1 on v0

--- a/solution.py
+++ b/solution.py
@@ -125,7 +125,7 @@
     local_target = jnp.sum(measured * measured)
     devices = lax.axis_size("row") * lax.axis_size("col")
     frame_count = frame_total * devices
-    totals, target_sum = lax.psum((probe_acc, local_target), ("row", "col"))
+    totals, target_sum = lax.psum(lax.psum((probe_acc, local_target), "col"), "row")
     stepped = probe + totals[0:2] / (totals[2] + regular)
     probe_power = jnp.sum(stepped * stepped)
     target = target_sum / frame_count

time: 519 us -> 453 us (0.87)
  waiting for transfers between devices: 269 us -> 209 us
  blocking collectives: 81.6 us -> 74.4 us
    psum x1 -> x2, waiting for transfers between devices: 254 us -> 193 us  [the longest x1 106 us: per_device(): lax.psum((probe_acc, local_target), 'col')]
    psum x1 -> x2, blocking collectives: 81.6 us -> 74.4 us  [the longest x1 43.6 us: per_device(): lax.psum(lax.psum((probe_acc, local_target), 'col'), 'row')]
  transfers between devices with their start and end apart: 9 -> 10, of which waited for: 6 -> 7; matrix products, arithmetic and copies ran while one was open for 1% -> 2% of each run, Pallas kernels for 0% -> 0%
where the time goes in v1:
time: 453 us; the launch traced here: 451 us
  waiting for transfers between devices  209 us (46%)
  blocking collectives  74.4 us (16%)
  local copies, waits for them, and re-layouts  44.8 us (10%)
  other arithmetic  43.5 us (10%)
  starting transfers between devices  24.2 us (5%)
  matrix products  23.4 us (5%)
  loops' own time  15.9 us (4%)
  between operations  15.6 us (3%)
    psum x1, waiting for transfers between devices, per_device(): lax.psum((probe_acc, local_target), 'col')  106 us
    psum x1, waiting for transfers between devices, per_device(): lax.psum(lax.psum((probe_acc, local_target), 'col'), 'row')  87.8 us
    psum x1, blocking collectives, per_device(): lax.psum(lax.psum((probe_acc, local_target), 'col'), 'row')  43.6 us
    dynamic_update_slice x4, local copies, waits for them, and re-layouts, visit(): lax.dynamic_update_slice(canvas, current + update, (anchor, offset[0], of...  33.4 us
    psum x1, blocking collectives, per_device(): lax.psum((probe_acc, local_target), 'col')  30.8 us
    another operation x1, loops' own time, per_device(): lax.fori_loop(0, frame_total, visit, (canvas_start, probe_start))  15.9 us
    dot_general x8, matrix products, transform(): mixed = jnp.dot(left_matrix, stacked, precision=lax.Precision.HIGHEST)  14.9 us
    add x4, other arithmetic, visit(): current + update  12.5 us
  transfers between devices with their start and end apart: 10, of which 7 were waited for; matrix products, arithmetic and copies ran while one was open for 2% of the time, Pallas kernels for 0%

profile of v1, /device:TPU:2, one launch (start us, length us, event | category | flops | bytes accessed | tf_op | source)
XLA Modules:
  0.0 450.6 jit_solution(6508113162330521939)
XLA Ops:
  8.2 5.1 %collective-permute-start = (f32[2,32,256]{2,1,0:T(8,128)S(1)}, f32[2,32,256]{2,1,0:T(8,128)S(1)}, u32[]{:S(2)}, u32[]{:S(2)}) collective-permute-start(f32[2,32,256]{2,1,0:T(8,128)S(1)} %get-tuple-element.258), channel_id=1, source_target_pairs={{0,16},{16,32},{32,48},{48,64},{64,80},{80,96},{96,112},{112,128},... | collective-permute-start | bytes 196616 | tf_op jit(solution)/shard_map/ppermute | solution.py:19
  18.4 2.5 collective-permute-done.1
  21.9 1.9 collective-permute-start.2
  23.8 3.6 collective-permute-start.3
  27.7 2.9 collective-permute-done.2
  32.3 2.4 pad_maximum_fusion.5
  36.0 107.5 %while.16 = (s32[]{:T(128)}, f32[3,320,320]{2,1,0:T(8,128)}, f32[3,256,256]{2,1,0:T(8,128)}, s32[4,2]{0,1:T(2,128)S(1)}, f32[2,256,256]{2,1,0:T(8,128)S(1)}, /*i...) while((s32[]{:T(128)}, f32[3,320,320]{2,1,0:T(8,128)}, ...), condition=%wide.region_1.2_spmd.clone, body=%wide.region_0.1_spmd.clone.sunk | while | flops 3225354240 | bytes 31064388 | solution.py:113
  41.8 1.9 convolution_bitcast_fusion.4
  45.9 1.9 convolution_bitcast_fusion.5
  51.4 2.9 maximum_add_fusion.3
  54.3 8.8 %dynamic_update_slice.9 = f32[3,320,320]{2,1,0:T(8,128)} dynamic-update-slice(f32[3,320,320]{2,1,0:T(8,128)} %get-tuple-element.377, f32[3,256,256]{2,1,0:T(8,128)S(1)} %get-tuple-element.360, s32[]{:T(128)} %constant.57.clone.1..sunk, s32[]{:T(128)S(6)} %select_n.61, s32[]{:T(128)S(6)} %select_n.62) | dynamic-update-slice | bytes 1572868 | tf_op jit(solution)/shard_map/while/body/eval_jaxpr/dynamic_update_slice | solution.py:108
  68.9 1.9 convolution_bitcast_fusion.4
  73.0 1.9 convolution_bitcast_fusion.5
  78.4 3.2 maximum_add_fusion.3
  81.6 8.5 %dynamic_update_slice.9 = f32[3,320,320]{2,1,0:T(8,128)} dynamic-update-slice(f32[3,320,320]{2,1,0:T(8,128)} %get-tuple-element.377, f32[3,256,256]{2,1,0:T(8,128)S(1)} %get-tuple-element.360, s32[]{:T(128)} %constant.57.clone.1..sunk, s32[]{:T(128)S(6)} %select_n.61, s32[]{:T(128)S(6)} %select_n.62) | dynamic-update-slice | bytes 1572868 | tf_op jit(solution)/shard_map/while/body/eval_jaxpr/dynamic_update_slice | solution.py:108
  96.0 1.9 convolution_bitcast_fusion.4
  100.1 1.9 convolution_bitcast_fusion.5
  105.5 3.2 maximum_add_fusion.3
  108.7 8.5 %dynamic_update_slice.9 = f32[3,320,320]{2,1,0:T(8,128)} dynamic-update-slice(f32[3,320,320]{2,1,0:T(8,128)} %get-tuple-element.377, f32[3,256,256]{2,1,0:T(8,128)S(1)} %get-tuple-element.360, s32[]{:T(128)} %constant.57.clone.1..sunk, s32[]{:T(128)S(6)} %select_n.61, s32[]{:T(128)S(6)} %select_n.62) | dynamic-update-slice | bytes 1572868 | tf_op jit(solution)/shard_map/while/body/eval_jaxpr/dynamic_update_slice | solution.py:108
  123.1 1.9 convolution_bitcast_fusion.4
  127.2 1.9 convolution_bitcast_fusion.5
  132.7 3.2 maximum_add_fusion.3
  135.8 7.6 %dynamic_update_slice.9 = f32[3,320,320]{2,1,0:T(8,128)} dynamic-update-slice(f32[3,320,320]{2,1,0:T(8,128)} %get-tuple-element.377, f32[3,256,256]{2,1,0:T(8,128)S(1)} %get-tuple-element.360, s32[]{:T(128)} %constant.57.clone.1..sunk, s32[]{:T(128)S(6)} %select_n.61, s32[]{:T(128)S(6)} %select_n.62) | dynamic-update-slice | bytes 1572868 | tf_op jit(solution)/shard_map/while/body/eval_jaxpr/dynamic_update_slice | solution.py:108
  144.5 5.3 %collective-permute-start.4 = (f32[3,32,320]{2,1,0:T(8,128)S(1)}, f32[3,32,320]{2,1,0:T(8,128)S(1)}, u32[]{:S(2)}, u32[]{:S(2)}) collective-permute-start(f32[3,32,320]{2,1,0:T(8,128)S(1)} %get-tuple-element.249), channel_id=1, source_target_pairs={{0,16},{16,32},{32,48},{48,64},{64,80},{80,96},{96,112},{112,128},... | collective-permute-start | bytes 368648 | tf_op jit(solution)/shard_map/ppermute | solution.py:30
  153.0 6.2 %collective-permute-done.5 = f32[3,32,320]{2,1,0:T(8,128)S(1)} collective-permute-done((f32[3,32,320]{2,1,0:T(8,128)S(1)}, f32[3,32,320]{2,1,0:T(8,128)S(1)}, u32[]{:S(2)}, u32[]{:S(2)}) %collective-permute-start.5) | collective-permute-done | bytes 122912 | tf_op jit(solution)/shard_map/ppermute | solution.py:30
  160.7 2.5 collective-permute-start.6
  163.3 3.0 collective-permute-start.7
  166.3 105.7 %all-reduce.7.cloned.1.call-done = f32[3,256,256]{2,1,0:T(8,128)} async-done(((f32[3,256,256]{2,1,0:T(8,128)}), f32[3,256,256]{2,1,0:T(8,128)}) %all-reduce.7.cloned.1.call-update) | async-done | bytes 786448 | tf_op jit(solution)/shard_map/psum | solution.py:128
  272.0 2.1 multiply_reduce_fusion
  274.1 30.8 %psum.30 = f32[]{:T(128)} all-reduce(f32[]{:T(128)} %multiply_reduce_fusion), channel_id=1, replica_groups=mesh['row'=16,'col'=16] {'col'}, use_global_device_ids=true, to_apply=%region_5.6 | all-reduce | flops 1 | bytes 8 | tf_op jit(solution)/shard_map/psum | solution.py:128
  305.0 43.6 %psum.31 = f32[]{:T(128)} all-reduce(f32[]{:T(128)} %psum.30), channel_id=1, replica_groups=mesh['row'=16,'col'=16] {'row'}, use_global_device_ids=true, to_apply=%region_6.7 | all-reduce | flops 1 | bytes 8 | tf_op jit(solution)/shard_map/psum | solution.py:128
  351.5 87.8 %all-reduce.9.cloned.1.call-done = f32[3,256,256]{2,1,0:T(8,128)} async-done(((f32[3,256,256]{2,1,0:T(8,128)}), f32[3,256,256]{2,1,0:T(8,128)}) %all-reduce.9.cloned.1.call-update) | async-done | bytes 786448 | tf_op jit(solution)/shard_map/psum | solution.py:128
  (101 shorter events, 52.7 us)
Async XLA Ops:
  7.2 11.2 %copy-start.2 = (f32[2,256,256]{2,1,0:T(8,128)S(1)}, f32[2,256,256]{2,1,0:T(8,128)}, u32[]{:S(2)}) copy-start(f32[2,256,256]{2,1,0:T(8,128)} %param.6) | copy-start | bytes 1572868
  7.2 264.8 %all-reduce.7.cloned.1.call-start = ((), (), s32[]{:S(2)}) async-start(), calls=%async_computation | async-start | bytes 1572864 | tf_op jit(solution)/shard_map/psum | solution.py:128
  8.2 10.2 %collective-permute-start = (f32[2,32,256]{2,1,0:T(8,128)S(1)}, f32[2,32,256]{2,1,0:T(8,128)S(1)}, u32[]{:S(2)}, u32[]{:S(2)}) collective-permute-start(f32[2,32,256]{2,1,0:T(8,128)S(1)} %get-tuple-element.258), channel_id=1, source_target_pairs={{0,16},{16,32},{32,48},{48,64},{64,80},{80,96},{96,112},{112,128},... | collective-permute-start | bytes 196616 | tf_op jit(solution)/shard_map/ppermute | solution.py:19
  13.3 7.7 %collective-permute-start.1 = (f32[2,32,256]{2,1,0:T(8,128)S(1)}, f32[2,32,256]{2,1,0:T(8,128)S(1)}, u32[]{:S(2)}, u32[]{:S(2)}) collective-permute-start(f32[2,32,256]{2,1,0:T(8,128)S(1)} %get-tuple-element.257), channel_id=1, source_target_pairs={{16,0},{32,16},{48,32},{64,48},{80,64},{96,80},{112,96},{128,112},... | collective-permute-start | bytes 196616 | tf_op jit(solution)/shard_map/ppermute | solution.py:22
  21.9 8.7 %collective-permute-start.2 = (f32[2,320,32]{2,1,0:T(8,128)}, f32[2,320,32]{2,1,0:T(8,128)}, u32[]{:S(2)}, u32[]{:S(2)}) collective-permute-start(f32[2,320,32]{2,1,0:T(8,128)} %get-tuple-element.255), channel_id=1, source_target_pairs={{0,1},{1,2},{2,3},{3,4},{4,5},{5,6},{6,7},{7,8},{8,9},{9,10},{10,1... | collective-permute-start | bytes 245768 | tf_op jit(solution)/shard_map/ppermute | solution.py:19
  23.8 8.5 %collective-permute-start.3 = (f32[2,320,32]{2,1,0:T(8,128)}, f32[2,320,32]{2,1,0:T(8,128)}, u32[]{:S(2)}, u32[]{:S(2)}) collective-permute-start(f32[2,320,32]{2,1,0:T(8,128)} %get-tuple-element.256), channel_id=1, source_target_pairs={{1,0},{2,1},{3,2},{4,3},{5,4},{6,5},{7,6},{8,7},{9,8},{10,9},{11,1... | collective-permute-start | bytes 245768 | tf_op jit(solution)/shard_map/ppermute | solution.py:22
  27.7 8.3 %copy-start = (f32[2,256,256]{2,1,0:T(8,128)S(1)}, f32[2,256,256]{2,1,0:T(8,128)}, u32[]{:S(2)}) copy-start(f32[2,256,256]{2,1,0:T(8,128)} %param.7) | copy-start | bytes 1572868
  27.7 8.3 %copy-start.5 = (s32[1,1,4,2]{2,3,1,0:T(2,128)S(1)}, s32[1,1,4,2]{2,3,1,0:T(2,128)}, u32[]{:S(2)}) copy-start(s32[1,1,4,2]{2,3,1,0:T(2,128)} %param.9) | copy-start | bytes 100
  48.9 1.2 copy-start.1
  76.0 1.2 copy-start.1
  103.1 1.2 copy-start.1
  130.2 1.2 copy-start.1
  143.5 295.8 %all-reduce.9.cloned.1.call-start = ((), (), s32[]{:S(2)}) async-start(), calls=%async_computation.1 | async-start | bytes 1572864 | tf_op jit(solution)/shard_map/psum | solution.py:128
  144.5 8.5 %collective-permute-start.4 = (f32[3,32,320]{2,1,0:T(8,128)S(1)}, f32[3,32,320]{2,1,0:T(8,128)S(1)}, u32[]{:S(2)}, u32[]{:S(2)}) collective-permute-start(f32[3,32,320]{2,1,0:T(8,128)S(1)} %get-tuple-element.249), channel_id=1, source_target_pairs={{0,16},{16,32},{32,48},{48,64},{64,80},{80,96},{96,112},{112,128},... | collective-permute-start | bytes 368648 | tf_op jit(solution)/shard_map/ppermute | solution.py:30
  149.9 9.3 %collective-permute-start.5 = (f32[3,32,320]{2,1,0:T(8,128)S(1)}, f32[3,32,320]{2,1,0:T(8,128)S(1)}, u32[]{:S(2)}, u32[]{:S(2)}) collective-permute-start(f32[3,32,320]{2,1,0:T(8,128)S(1)} %get-tuple-element.250), channel_id=1, source_target_pairs={{16,0},{32,16},{48,32},{64,48},{80,64},{96,80},{112,96},{128,112},... | collective-permute-start | bytes 368648 | tf_op jit(solution)/shard_map/ppermute | solution.py:30
  160.7 188.5 %collective-permute-start.6 = (f32[3,256,32]{2,1,0:T(8,128)S(1)}, f32[3,256,32]{2,1,0:T(8,128)S(1)}, u32[]{:S(2)}, u32[]{:S(2)}) collective-permute-start(f32[3,256,32]{2,1,0:T(8,128)S(1)} %get-tuple-element.251), channel_id=1, source_target_pairs={{0,1},{1,2},{2,3},{3,4},{4,5},{5,6},{6,7},{7,8},{8,9},{9,10},{10,1... | collective-permute-start | bytes 294920 | tf_op jit(solution)/shard_map/ppermute | solution.py:30
  163.3 185.9 %collective-permute-start.7 = (f32[3,256,32]{2,1,0:T(8,128)S(1)}, f32[3,256,32]{2,1,0:T(8,128)}, u32[]{:S(2)}, u32[]{:S(2)}) collective-permute-start(f32[3,256,32]{2,1,0:T(8,128)S(1)} %get-tuple-element.252), channel_id=1, source_target_pairs={{1,0},{2,1},{3,2},{4,3},{5,4},{6,5},{7,6},{8,7},{9,8},{10,9},{11,1... | collective-permute-start | bytes 294920 | tf_op jit(solution)/shard_map/ppermute | solution.py:30
  274.1 76.5 %copy-start.3 = (f32[2,256,256]{2,1,0:T(8,128)S(1)}, f32[2,256,256]{2,1,0:T(8,128)}, u32[]{:S(2)}) copy-start(f32[2,256,256]{2,1,0:T(8,128)} %param.6) | copy-start | bytes 1572868
  439.3 3.6 copy-start.4
Sparse Core Ops, SparseCore 0:
  143.6 128.3 all-reduce.6
  274.6 164.6 all-reduce.8
